TPU v7x, 32 devices: a whole 2x2x4 slice. The times are simulated.
32 devices in a mesh: groups: 2 (over x), frames: 16 (over z, y, core).
Axes of the slice: x: 2, y: 2, z: 4, core: 2. Of those that a mesh axis runs over, the one named last changes fastest.
Arguments:
- video: float32 [4, 16, 256, 256], P('groups', 'frames'), parts along dimension 0, may hold values from -9 to 9
- clip_start: int32 [4], P('groups'), parts along dimension 0, may hold values from 0 to 7
- gain_space: float32 [256], replicated, may hold values from 0.1 to 1.9
- qkv_space: float32 [256, 768], replicated, may hold values from -0.375 to 0.375
- out_space: float32 [256, 256], replicated, may hold values from -0.375 to 0.375
- gain_time: float32 [256], replicated, may hold values from 0.1 to 1.9
- qkv_time: float32 [256, 768], replicated, may hold values from -0.375 to 0.375
- out_time: float32 [256, 256], replicated, may hold values from -0.375 to 0.375
- code_sums: float32 [8192, 256], P(('groups', 'frames')), parts along dimension 0, may hold values from -12 to 12
- code_counts: float32 [8192], P(('groups', 'frames')), parts along dimension 0, may hold values from 1 to 10
Outputs:
- latents: float32 [4, 16, 256, 256], P('groups', None, 'frames'), parts along dimension 0
- new_sums: float32 [8192, 256], P(('groups', 'frames')), parts along dimension 0
- new_counts: float32 [8192], P(('groups', 'frames')), parts along dimension 0
- new_codebook: float32 [8192, 256], P(('groups', 'frames')), parts along dimension 0
There are 2 independent parts, one for each index of `groups`. A program takes and returns all parts, laid end to end along the dimension named above; an argument that names none is the same for every part. Nothing has to cross between parts.
All inputs are finite; a program needn't handle non-finite values.
Results may differ from a plain program's by a relative error of at most 0.0003.
Values sent between devices are 32-bit elements; how exact they have to be, the bound alone decides.
A program may use at most 64 MiB of HBM per device.

v0:
```python
import jax
import jax.numpy as jnp
from jax import lax
from jax.sharding import PartitionSpec as P

HEADS = 4
ATTN_SCALE = 10.0
SOFTMAX_WARMTH = 0.05
DECAY_RATE = 0.9
EPSILON = 1e-06
TOP_PRECISION = lax.Precision.HIGHEST


def rms_norm(values, gain_vec):
    return values * lax.rsqrt(jnp.mean(values * values, -1, keepdims=True) + EPSILON) * gain_vec


def unit_vec(values):
    return values * lax.rsqrt(jnp.sum(values * values, -1, keepdims=True) + EPSILON)


def spatial_block(one_frame, gain_vec, w_qkv, w_out):
    width = one_frame.shape[-1]
    normed = rms_norm(one_frame, gain_vec)
    packed = jnp.dot(normed, w_qkv, precision=TOP_PRECISION)
    queries = unit_vec(packed[:, :width].reshape(-1, HEADS, width // HEADS))
    key_vecs = unit_vec(packed[:, width : 2 * width].reshape(-1, HEADS, width // HEADS))
    values = packed[:, 2 * width :].reshape(-1, HEADS, width // HEADS)
    scores = ATTN_SCALE * jnp.einsum("qhd,khd->hqk", queries, key_vecs, precision=TOP_PRECISION)
    assignment_weights = jnp.exp(scores)
    totals = jnp.sum(assignment_weights, -1).T[:, :, None]
    mixed = jnp.einsum("hqk,khd->qhd", assignment_weights, values, precision=TOP_PRECISION) / totals
    return one_frame + jnp.dot(mixed.reshape(-1, width), w_out, precision=TOP_PRECISION)


def time_block(spaced, clip_start, gain_vec, w_qkv, w_out):
    clips, frames, places, width = spaced.shape
    normed = rms_norm(spaced, gain_vec)
    packed = jnp.einsum("ctpd,de->ctpe", normed, w_qkv, precision=TOP_PRECISION)
    shape_heads = (clips, frames, places, HEADS, width // HEADS)
    queries = unit_vec(packed[..., :width].reshape(shape_heads))
    key_vecs = unit_vec(packed[..., width : 2 * width].reshape(shape_heads))
    values = packed[..., 2 * width :].reshape(shape_heads)
    scores = ATTN_SCALE * jnp.einsum(
        "ctphd,csphd->cphts", queries, key_vecs, precision=TOP_PRECISION
    )
    later = jnp.arange(frames, dtype=jnp.int32)[:, None]
    earlier = jnp.arange(frames, dtype=jnp.int32)[None, :]
    allowed = (earlier <= later)[None] & (
        (earlier[None] >= clip_start[:, None, None]) | (earlier == later)[None]
    )
    assignment_weights = jnp.exp(scores) * allowed[:, None, None, :, :].astype(jnp.float32)
    totals = jnp.transpose(jnp.sum(assignment_weights, -1), (0, 3, 1, 2))[..., None]
    mixed = (
        jnp.einsum("cphts,csphd->ctphd", assignment_weights, values, precision=TOP_PRECISION)
        / totals
    )
    return spaced + jnp.einsum(
        "ctpd,de->ctpe", mixed.reshape(clips, frames, places, width), w_out, precision=TOP_PRECISION
    )


def local(
    video,
    clip_start,
    gain_space,
    qkv_space,
    out_space,
    gain_time,
    qkv_time,
    out_time,
    code_sums,
    code_counts,
):
    clips, local_frames, places, width = video.shape
    flat_frames = video.reshape(clips * local_frames, places, width)
    spaced = lax.map(
        lambda one_frame: spatial_block(one_frame, gain_space, qkv_space, out_space), flat_frames
    )
    spaced = spaced.reshape(clips, local_frames, places, width)
    by_place = lax.all_to_all(spaced, "frames", split_axis=2, concat_axis=1, tiled=True)
    latents = time_block(by_place, clip_start, gain_time, qkv_time, out_time)
    unit_token_vectors = unit_vec(latents.reshape(-1, width))
    local_codes = unit_vec(code_sums / code_counts[:, None])
    codebook_matrix = lax.all_gather(local_codes, "frames", axis=0, tiled=True)
    assignment_weights = jnp.exp(
        jnp.dot(unit_token_vectors, codebook_matrix.T, precision=TOP_PRECISION) / SOFTMAX_WARMTH
    )
    probs = assignment_weights / jnp.sum(assignment_weights, 1, keepdims=True)
    term_sums = lax.dot_general(
        probs, unit_token_vectors, (((0,), (0,)), ((), ())), precision=TOP_PRECISION
    )
    term_counts = jnp.sum(probs, 0)
    got_sums, got_counts = (
        lax.psum_scatter(term_sums, "frames", scatter_dimension=0, tiled=True),
        lax.psum_scatter(term_counts, "frames", scatter_dimension=0, tiled=True),
    )
    new_sums = DECAY_RATE * code_sums + (1.0 - DECAY_RATE) * got_sums
    new_counts = DECAY_RATE * code_counts + (1.0 - DECAY_RATE) * got_counts
    new_codebook = new_sums / new_counts[:, None]
    return (latents, new_sums, new_counts, new_codebook)


def solution(mesh):
    in_specs = (
        P("groups", "frames", None, None),
        P("groups"),
        P(),
        P(),
        P(),
        P(),
        P(),
        P(),
        P(("groups", "frames"), None),
        P(("groups", "frames")),
    )
    out_specs = (
        P("groups", None, "frames", None),
        P(("groups", "frames"), None),
        P(("groups", "frames")),
        P(("groups", "frames"), None),
    )
    return jax.shard_map(local, mesh=mesh, in_specs=in_specs, out_specs=out_specs, check_vma=False)
```

profile of v0, /device:TPU:0, one launch (start us, length us, event | category | flops | bytes accessed | tf_op | source)
XLA Modules:
  0.0 198.9 jit_solution(9034979632726046601)
XLA Ops:
  7.2 1.2 multiply_reduce_fusion.6
  8.4 1.8 broadcast_multiply_fusion.2
  10.3 25.9 %while.10 = (s32[]{:T(128)}, f32[2,256,256]{2,0,1:T(2,128)}, f32[2,256,256]{2,1,0:T(8,128)}, f32[256]{0:T(256)}, f32[256,768]{1,0:T(8,128)}, /*index=5*/f32[256,256]{1,0:T(8,128)}, s32[]{:T(128)}, s32[]{:T(128)}) while((s32[]{:T(128)}, f32[2,256,256]{2,0,1:T(2,128)}, f32[2,256,256]{2,1,0:T(8,128)}, f32[256]{0:T(256)}, f32[256,768]{1,0:T(8,128)}, ...), condition=%wide.region_5.6_spmd, body=%wide.region_0.5_spmd.sunk | while | flops 1209269504 | bytes 14202521 | solution.py:77
  11.5 2.1 %fusion.68 = f32[256,768]{1,0:T(8,128)S(1)} fusion(f32[256,768]{1,0:T(8,128)} %get-tuple-element.142, f32[2,256,256]{2,1,0:T(8,128)} %get-tuple-element.140, s32[]{:T(128)} %get-tuple-element.130, f32[256]{0:T(256)} %get-tuple-element.141, f32[256]{0:T(256)S(1)} %add_rsqrt_fusion.10), kind=kOutput, calls=%fused_computation.10.clone.1 | convolution fusion | flops 604110848 | bytes 1837568 | tf_op jit(solution)/shard_map/while/body/eval_jaxpr/dot_general | solution.py:25
  16.9 6.3 %dynamic_update_slice.5 = f32[2,256,256]{2,0,1:T(2,128)} dynamic-update-slice(f32[2,256,256]{2,0,1:T(2,128)} %get-tuple-element.131, f32[1,256,256]{2,0,1:T(1,128)S(1)} %copy.85, s32[]{:T(128)} %get-tuple-element.130, s32[]{:T(128)} %constant.22.clone.1..sunk, s32[]{:T(128)} %constant.22.clone.1..sunk) | dynamic-update-slice | bytes 524292 | tf_op jit(solution)/shard_map/while/body/jit(dynamic_update_index_in_dim)/dynamic_update_slice | solution.py:77
  24.4 2.1 %fusion.68 = f32[256,768]{1,0:T(8,128)S(1)} fusion(f32[256,768]{1,0:T(8,128)} %get-tuple-element.142, f32[2,256,256]{2,1,0:T(8,128)} %get-tuple-element.140, s32[]{:T(128)} %get-tuple-element.130, f32[256]{0:T(256)} %get-tuple-element.141, f32[256]{0:T(256)S(1)} %add_rsqrt_fusion.10), kind=kOutput, calls=%fused_computation.10.clone.1 | convolution fusion | flops 604110848 | bytes 1837568 | tf_op jit(solution)/shard_map/while/body/eval_jaxpr/dot_general | solution.py:25
  29.9 6.3 %dynamic_update_slice.5 = f32[2,256,256]{2,0,1:T(2,128)} dynamic-update-slice(f32[2,256,256]{2,0,1:T(2,128)} %get-tuple-element.131, f32[1,256,256]{2,0,1:T(1,128)S(1)} %copy.85, s32[]{:T(128)} %get-tuple-element.130, s32[]{:T(128)} %constant.22.clone.1..sunk, s32[]{:T(128)} %constant.22.clone.1..sunk) | dynamic-update-slice | bytes 524292 | tf_op jit(solution)/shard_map/while/body/jit(dynamic_update_index_in_dim)/dynamic_update_slice | solution.py:77
  36.2 7.4 %all-to-all-start = ((f32[2,1,256,256]{3,0,1,2:T(2,128)}), f32[2,1,256,256]{3,0,1,2:T(2,128)S(1)}, u32[]{:S(2)}, u32[]{:S(2)}) async-start(f32[2,1,256,256]{3,0,1,2:T(2,128)} %bitcast.103), calls=%async_computation | async-start | bytes 1048576 | tf_op jit(solution)/shard_map/all_to_all | solution.py:81
  43.8 22.8 %all-to-all-done = f32[2,1,256,256]{3,0,1,2:T(2,128)S(1)} async-done(((f32[2,1,256,256]{3,0,1,2:T(2,128)}), f32[2,1,256,256]{3,0,1,2:T(2,128)S(1)}, u32[]{:S(2)}, u32[]{:S(2)}) %all-to-all-start) | async-done | bytes 524320 | tf_op jit(solution)/shard_map/all_to_all | solution.py:81
  67.3 1.5 fusion.23
  68.8 1.2 fusion.37
  70.4 1.5 reshape.171
  71.9 2.5 %reshape.170 = f32[2,16,16,4,64]{4,3,2,1,0:T(4,128)} reshape(f32[2,16,16,256]{3,2,1,0:T(8,128)} %get-tuple-element.58) | data formatting | bytes 1048576 | tf_op jit(solution)/shard_map/reshape | solution.py:43
  75.7 1.5 broadcast_multiply_fusion
  77.1 3.1 %fusion.38 = (f32[2,16,4,16]{3,2,1,0:T(4,128)S(1)}, f32[2,16,4,16,16]{3,4,2,1,0:T(8,128)S(1)}) fusion(f32[2,16,16]{1,2,0:T(8,128)S(1)} %and_convert_fusion, f32[2,16,16,4,64]{4,3,2,1,0:T(4,128)S(1)} %get-tuple-element.69, f32[2,16,16,4,64]{4,3,2,1,0:T(4,128)S(1)} %get-tuple-element.70), kind=kOutput, calls=%fused_computation.72 | convolution fusion | flops 25262080 | bytes 1189888 | tf_op jit(solution)/shard_map/ctphd,csphd->cphts/dot_general | solution.py:44
  80.3 2.5 %fusion.17 = f32[2,16,16,4,64]{4,1,3,2,0:T(8,128)S(1)} fusion(f32[2,16,4,16,16]{3,4,2,1,0:T(8,128)S(1)} %get-tuple-element.62, f32[2,16,16,4,64]{4,3,2,1,0:T(4,128)S(1)} %copy-done.6, f32[2,16,16,4]{1,3,2,0:T(4,128)S(1)} %bitcast.106), kind=kOutput, calls=%fused_computation.28 | convolution fusion | flops 25296896 | bytes 1187840 | tf_op jit(solution)/shard_map/cphts,csphd->ctphd/dot_general | solution.py:55
  83.9 1.6 multiply_reduce_fusion.4
  85.8 9.9 %fusion.16 = (f32[512]{0:T(512)S(1)}, f32[512,4096]{1,0:T(8,128)S(1)}) fusion(f32[512,256]{1,0:T(8,128)S(1)} %bitcast_multiply_fusion.2, f32[4096,256]{1,0:T(8,128)} %all-gather.2.cloned.1.call-done), kind=kOutput, calls=%fused_computation.26 | convolution fusion | flops 6446644736 | bytes 13109248 | tf_op jit(solution)/shard_map/dot_general | solution.py:87
  95.7 3.2 %copy-done.1 = f32[512,4096]{1,0:T(8,128)} copy-done((f32[512,4096]{1,0:T(8,128)}, f32[512,4096]{1,0:T(8,128)S(1)}, u32[]{:S(2)}) %copy-start.1) | copy-done | bytes 8388632
  98.9 15.0 %fusion.28 = f32[4096,256]{1,0:T(8,128)} fusion(f32[512,256]{1,0:T(8,128)S(1)} %bitcast_multiply_fusion.2, f32[512,4096]{1,0:T(8,128)S(1)} %get-tuple-element.66, f32[512]{0:T(512)S(1)} %get-tuple-element.65), kind=kOutput, calls=%fused_computation.48 | convolution fusion | flops 6446645248 | bytes 13109248 | tf_op jit(solution)/shard_map/dot_general | solution.py:90
  115.2 4.3 %fusion.27 = f32[4096]{0:T(1024)S(1)} fusion(f32[512]{0:T(512)S(1)} %get-tuple-element.65, f32[512,4096]{1,0:T(8,128)} %copy-done.1), kind=kLoop, calls=%fused_computation.47 | loop fusion | flops 6287360 | bytes 8407040 | tf_op jit(solution)/shard_map/reduce_sum | solution.py:93
  119.5 64.5 %all-reduce = f32[4096]{0:T(1024)S(1)} all-reduce(f32[4096]{0:T(1024)S(1)} %fusion.27), channel_id=3, replica_groups=mesh['groups'=2,'frames'=16] {'frames'}, use_global_device_ids=true, to_apply=%region_15.16.clone | all-reduce | flops 4096 | bytes 32768
  184.1 6.2 %reduce-scatter.2.cloned.1.call-done = f32[256,256]{1,0:T(8,128)} async-done(((f32[4096,256]{1,0:T(8,128)}), f32[256,256]{1,0:T(8,128)}) %reduce-scatter.2.cloned.1.call-update) | async-done | bytes 262160 | tf_op jit(solution)/shard_map/reduce_scatter | solution.py:95
  190.3 1.8 broadcast_divide_fusion
  (79 shorter events, 13.5 us)
Async XLA Ops:
  7.2 60.1 %copy-start = (f32[256,768]{1,0:T(8,128)S(1)}, f32[256,768]{1,0:T(8,128)}, u32[]{:S(2)}) copy-start(f32[256,768]{1,0:T(8,128)} %param.18) | copy-start | bytes 2359300
  7.2 78.6 %all-gather.2.cloned.1.call-start = ((), (), s32[]{:S(2)}) async-start(), calls=%async_computation.2 | async-start | bytes 4456448 | tf_op jit(solution)/shard_map/all_gather | solution.py:85
  10.3 33.4 %copy-start.10 = (s32[2]{0:T(128)S(1)}, s32[2]{0:T(128)}, u32[]{:S(2)}) copy-start(s32[2]{0:T(128)} %param.13) | copy-start | bytes 28
  10.3 57.0 %copy-start.9 = (f32[256]{0:T(256)S(1)}, f32[256]{0:T(256)}, u32[]{:S(2)}) copy-start(f32[256]{0:T(256)} %param.17) | copy-start | bytes 3076
  10.3 5.7 %copy-start.2 = (f32[2,256,256]{2,1,0:T(8,128)S(1)}, f32[2,256,256]{2,1,0:T(8,128)}, u32[]{:S(2)}) copy-start(f32[2,256,256]{2,1,0:T(8,128)} %get-tuple-element.140) | copy-start | bytes 1572868 | tf_op jit(solution)/shard_map/while
  10.3 5.7 %copy-start.3 = (f32[256,256]{1,0:T(8,128)S(1)}, f32[256,256]{1,0:T(8,128)}, u32[]{:S(2)}) copy-start(f32[256,256]{1,0:T(8,128)} %get-tuple-element.143) | copy-start | bytes 786436 | tf_op jit(solution)/shard_map/while
  23.3 5.7 %copy-start.2 = (f32[2,256,256]{2,1,0:T(8,128)S(1)}, f32[2,256,256]{2,1,0:T(8,128)}, u32[]{:S(2)}) copy-start(f32[2,256,256]{2,1,0:T(8,128)} %get-tuple-element.140) | copy-start | bytes 1572868 | tf_op jit(solution)/shard_map/while
  23.3 5.7 %copy-start.3 = (f32[256,256]{1,0:T(8,128)S(1)}, f32[256,256]{1,0:T(8,128)}, u32[]{:S(2)}) copy-start(f32[256,256]{1,0:T(8,128)} %get-tuple-element.143) | copy-start | bytes 786436 | tf_op jit(solution)/shard_map/while
  36.2 30.5 %all-to-all-start = ((f32[2,1,256,256]{3,0,1,2:T(2,128)}), f32[2,1,256,256]{3,0,1,2:T(2,128)S(1)}, u32[]{:S(2)}, u32[]{:S(2)}) async-start(f32[2,1,256,256]{3,0,1,2:T(2,128)} %bitcast.103), calls=%async_computation | async-start | bytes 1048576 | tf_op jit(solution)/shard_map/all_to_all | solution.py:81
  43.6 146.7 %reduce-scatter.2.cloned.1.call-start = ((), (), s32[]{:S(2)}) async-start(), calls=%async_computation.3 | async-start | bytes 4456448 | tf_op jit(solution)/shard_map/reduce_scatter | solution.py:95
  74.3 6.0 %copy-start.6 = (f32[2,16,16,4,64]{4,3,2,1,0:T(4,128)S(1)}, f32[2,16,16,4,64]{4,3,2,1,0:T(4,128)}, u32[]{:S(2)}) copy-start(f32[2,16,16,4,64]{4,3,2,1,0:T(4,128)} %reshape.170) | copy-start | bytes 1572868
  85.5 28.5 %copy-start.5 = (f32[2,16,16,256]{3,2,1,0:T(8,128)}, f32[2,16,16,256]{3,2,1,0:T(8,128)S(1)}, u32[]{:S(2)}) copy-start(f32[2,16,16,256]{3,2,1,0:T(8,128)S(1)} %get-tuple-element.64) | copy-start | bytes 1572868
  95.7 3.2 %copy-start.1 = (f32[512,4096]{1,0:T(8,128)}, f32[512,4096]{1,0:T(8,128)S(1)}, u32[]{:S(2)}) copy-start(f32[512,4096]{1,0:T(8,128)S(1)} %get-tuple-element.66) | copy-start | bytes 25165828
  98.9 15.1 %copy-start.11 = (u32[32]{0:T(128)S(1)}, u32[32]{0:T(128)}, u32[]{:S(2)}) copy-start(u32[32]{0:T(128)} %constant.46) | copy-start | bytes 388
  114.0 70.1 %copy-start.7 = (f32[256]{0:T(256)S(1)}, f32[256]{0:T(256)}, u32[]{:S(2)}) copy-start(f32[256]{0:T(256)} %param.21) | copy-start | bytes 3076
  114.0 76.3 %copy-start.4 = (f32[256,256]{1,0:T(8,128)S(1)}, f32[256,256]{1,0:T(8,128)}, u32[]{:S(2)}) copy-start(f32[256,256]{1,0:T(8,128)} %param.20) | copy-start | bytes 786436
  184.1 8.0 %copy-start.8 = (f32[256]{0:T(256)}, f32[256]{0:T(256)S(1)}, u32[]{:S(2)}) copy-start(f32[256]{0:T(256)S(1)} %fusion.33) | copy-start | bytes 3076
Sparse Core Ops, SparseCore 0:
  10.7 62.2 all-gather.1
  114.1 76.1 reduce-scatter.1
where the time goes:
time: 200 us; the launch traced here: 199 us
  blocking collectives  64.5 us (32%)
  matrix products  42.9 us (21%)
  waiting for transfers between devices  29.1 us (15%)
  local copies, waits for them, and re-layouts  24.8 us (12%)
  other arithmetic  15 us (8%)
  between operations  14.9 us (7%)
  starting transfers between devices  7.5 us (4%)
    unnamed x1, blocking collectives  64.5 us
    all_to_all x1, waiting for transfers between devices, local(): lax.all_to_all(spaced, 'frames', split_axis=2, concat_axis=1, tiled=True)  22.8 us
    dot_general x1, matrix products, local(): lax.dot_general(probs, unit_token_vectors, (((0,), (0,)), ((), ())), prec...  15 us
    dynamic_update_slice x4, local copies, waits for them, and re-layouts, local(): lax.map(lambda one_frame: spatial_block(one_frame, gain_space, qkv_space,...  13.2 us
    dot_general x1, matrix products, local(): jnp.dot(unit_token_vectors, codebook_matrix.T, precision=TOP_PRECISION)  9.91 us
    all_to_all x1, starting transfers between devices, local(): lax.all_to_all(spaced, 'frames', split_axis=2, concat_axis=1, tiled=True)  7.42 us
    reduce_scatter x1, waiting for transfers between devices, local(): lax.psum_scatter(term_sums, 'frames', scatter_dimension=0, tiled=True)  6.17 us
    reduce_sum x1, other arithmetic, local(): term_counts = jnp.sum(probs, 0)  4.27 us
  transfers between devices with their start and end apart: 3, of which 2 were waited for; matrix products, arithmetic and copies ran while one was open for 25% of the time, Pallas kernels for 0%

commit v1 on v0

--- a/solution.py
+++ b/solution.py
@@ -9,6 +9,18 @@
 DECAY_RATE = 0.9
 EPSILON = 1e-06
 TOP_PRECISION = lax.Precision.HIGHEST
+
+
+def cut_along(x, dim, peers):
+    dims = x.shape
+    blocks = x.reshape(*dims[:dim], peers, dims[dim] // peers, *dims[dim + 1 :])
+    return jnp.moveaxis(blocks, dim, 0)
+
+
+def in_order(pieces, dim):
+    shape = list(pieces.shape[1:])
+    shape[dim] *= pieces.shape[0]
+    return jnp.moveaxis(pieces, 0, dim).reshape(shape)
 
 
 def rms_norm(values, gain_vec):
@@ -78,7 +90,16 @@
         lambda one_frame: spatial_block(one_frame, gain_space, qkv_space, out_space), flat_frames
     )
     spaced = spaced.reshape(clips, local_frames, places, width)
-    by_place = lax.all_to_all(spaced, "frames", split_axis=2, concat_axis=1, tiled=True)
+    devices, position = (lax.axis_size("frames"), lax.axis_index("frames"))
+    pieces = cut_along(spaced, 2, devices)
+    outs = [pieces[position]]
+    for lap in range(1, devices):
+        sent = pieces[(position + lap) % devices]
+        outs.append(
+            lax.ppermute(sent, "frames", [(i, (i + lap) % devices) for i in range(devices)])
+        )
+    pieces = jnp.stack(outs)[(position - jnp.arange(devices)) % devices]
+    by_place = in_order(pieces, 1)
     latents = time_block(by_place, clip_start, gain_time, qkv_time, out_time)
     unit_token_vectors = unit_vec(latents.reshape(-1, width))
     local_codes = unit_vec(code_sums / code_counts[:, None])

time: 200 us -> 191 us (0.955)
  starting transfers between devices: 7.5 us -> 29.4 us
  waiting for transfers between devices: 29.1 us -> 9.02 us
  local copies, waits for them, and re-layouts: 24.8 us -> 13.9 us
    ppermute x0 -> x15, starting transfers between devices: none -> 29.3 us  [local(): lax.ppermute(sent, 'frames', [(i, (i + lap) % devices) for i in range(dev...]
    all_to_all x1 -> x0, waiting for transfers between devices: 22.8 us -> none  [local(): lax.all_to_all(spaced, 'frames', split_axis=2, concat_axis=1, tiled=True)]
    dynamic_update_slice x4 -> x0, local copies, waits for them, and re-layouts: 13.2 us -> none  [local(): lax.map(lambda one_frame: spatial_block(one_frame, gain_space, qkv_space,...]
    all_to_all x1 -> x0, starting transfers between devices: 7.42 us -> none  [local(): lax.all_to_all(spaced, 'frames', split_axis=2, concat_axis=1, tiled=True)]
    ppermute x0 -> x15, waiting for transfers between devices: none -> 2.58 us  [local(): lax.ppermute(sent, 'frames', [(i, (i + lap) % devices) for i in range(dev...]
    unnamed x21 -> x36, local copies, waits for them, and re-layouts: 3.85 us -> 4.67 us
  transfers between devices with their start and end apart: 3 -> 17, of which waited for: 2 -> 3; matrix products, arithmetic and copies ran while one was open for 25% -> 21% of each run, Pallas kernels for 0% -> 0%
where the time goes in v1:
time: 191 us; the launch traced here: 190 us
  blocking collectives  63.3 us (33%)
  matrix products  44.3 us (23%)
  starting transfers between devices  29.4 us (15%)
  between operations  15.2 us (8%)
  other arithmetic  14.8 us (8%)
  local copies, waits for them, and re-layouts  13.9 us (7%)
  waiting for transfers between devices  9.02 us (5%)
    unnamed x1, blocking collectives  63.3 us
    ppermute x15, starting transfers between devices, local(): lax.ppermute(sent, 'frames', [(i, (i + lap) % devices) for i in range(dev...  29.3 us
    dot_general x1, matrix products, local(): lax.dot_general(probs, unit_token_vectors, (((0,), (0,)), ((), ())), prec...  15.1 us
    dot_general x1, matrix products, local(): jnp.dot(unit_token_vectors, codebook_matrix.T, precision=TOP_PRECISION)  9.91 us
    reduce_scatter x1, waiting for transfers between devices, local(): lax.psum_scatter(term_sums, 'frames', scatter_dimension=0, tiled=True)  6.39 us
    unnamed x36, local copies, waits for them, and re-layouts  4.67 us
    reduce_sum x1, other arithmetic, local(): term_counts = jnp.sum(probs, 0)  4.27 us
    dot_general x2, matrix products, spatial_block(): packed = jnp.dot(normed, w_qkv, precision=TOP_PRECISION)  4.17 us
  transfers between devices with their start and end apart: 17, of which 3 were waited for; matrix products, arithmetic and copies ran while one was open for 21% of the time, Pallas kernels for 0%

profile of v1, /device:TPU:0, one launch (start us, length us, event | category | flops | bytes accessed | tf_op | source)
XLA Modules:
  0.0 190.1 jit_solution(1780441460441530563)
XLA Ops:
  8.4 1.8 broadcast_multiply_fusion.2
  10.5 14.1 %while.10 = (s32[]{:T(128)}, f32[2,256,256]{2,1,0:T(8,128)}, f32[2,256,256]{2,1,0:T(8,128)}, f32[256]{0:T(256)}, f32[256,768]{1,0:T(8,128)}, /*index=5*/f32[256,256]{1,0:T(8,128)}, s32[]{:T(128)}) while((s32[]{:T(128)}, f32[2,256,256]{2,1,0:T(8,128)}, f32[2,256,256]{2,1,0:T(8,128)}, f32[256]{0:T(256)}, f32[256,768]{1,0:T(8,128)}, ...), condition=%wide.region_5.6_spmd, body=%wide.region_0.5_spmd.sunk | while | flops 1209269504 | bytes 13154441 | solution.py:89
  11.7 2.1 %fusion.73 = f32[256,768]{1,0:T(8,128)S(1)} fusion(f32[256,768]{1,0:T(8,128)} %get-tuple-element.155, f32[2,256,256]{2,1,0:T(8,128)} %get-tuple-element.153, s32[]{:T(128)} %get-tuple-element.144, f32[256]{0:T(256)} %get-tuple-element.154, f32[256]{0:T(256)S(1)} %add_rsqrt_fusion.10), kind=kOutput, calls=%fused_computation.12.clone.1 | convolution fusion | flops 604110848 | bytes 1837568 | tf_op jit(solution)/shard_map/while/body/eval_jaxpr/dot_general | solution.py:37
  18.7 2.1 %fusion.73 = f32[256,768]{1,0:T(8,128)S(1)} fusion(f32[256,768]{1,0:T(8,128)} %get-tuple-element.155, f32[2,256,256]{2,1,0:T(8,128)} %get-tuple-element.153, s32[]{:T(128)} %get-tuple-element.144, f32[256]{0:T(256)} %get-tuple-element.154, f32[256]{0:T(256)S(1)} %add_rsqrt_fusion.10), kind=kOutput, calls=%fused_computation.12.clone.1 | convolution fusion | flops 604110848 | bytes 1837568 | tf_op jit(solution)/shard_map/while/body/eval_jaxpr/dot_general | solution.py:37
  26.2 2.6 %collective-permute-start.1 = (f32[2,1,16,256]{3,2,0,1:T(8,128)S(1)}, f32[2,1,16,256]{3,2,0,1:T(8,128)S(1)}, u32[]{:S(2)}, u32[]{:S(2)}) collective-permute-start(f32[2,1,16,256]{3,2,0,1:T(8,128)S(1)} %get-tuple-element.74), channel_id=1, source_target_pairs={{0,2},{1,3},{2,4},{3,5},{4,6},{5,7},{6,8},{7,9},{8,10},{9,11},{10,... | collective-permute-start | bytes 98312 | tf_op jit(solution)/shard_map/ppermute | solution.py:99
  28.8 2.4 %collective-permute-start.2 = (f32[2,1,16,256]{3,2,0,1:T(8,128)S(1)}, f32[2,1,16,256]{3,2,0,1:T(8,128)S(1)}, u32[]{:S(2)}, u32[]{:S(2)}) collective-permute-start(f32[2,1,16,256]{3,2,0,1:T(8,128)S(1)} %get-tuple-element.73), channel_id=1, source_target_pairs={{0,3},{1,4},{2,5},{3,6},{4,7},{5,8},{6,9},{7,10},{8,11},{9,12},{10... | collective-permute-start | bytes 98312 | tf_op jit(solution)/shard_map/ppermute | solution.py:99
  35.2 4.3 %collective-permute-start.6 = (f32[2,1,16,256]{3,2,0,1:T(8,128)S(1)}, f32[2,1,16,256]{3,2,0,1:T(8,128)S(1)}, u32[]{:S(2)}, u32[]{:S(2)}) collective-permute-start(f32[2,1,16,256]{3,2,0,1:T(8,128)S(1)} %get-tuple-element.69), channel_id=1, source_target_pairs={{0,7},{1,8},{2,9},{3,10},{4,11},{5,12},{6,13},{7,14},{8,15},{9,0},... | collective-permute-start | bytes 98312 | tf_op jit(solution)/shard_map/ppermute | solution.py:99
  40.2 2.4 %collective-permute-start.9 = (f32[2,1,16,256]{3,2,0,1:T(8,128)S(1)}, f32[2,1,16,256]{3,2,0,1:T(8,128)S(1)}, u32[]{:S(2)}, u32[]{:S(2)}) collective-permute-start(f32[2,1,16,256]{3,2,0,1:T(8,128)S(1)} %get-tuple-element.66), channel_id=1, source_target_pairs={{0,10},{1,11},{2,12},{3,13},{4,14},{5,15},{6,0},{7,1},{8,2},{9,3},... | collective-permute-start | bytes 98312 | tf_op jit(solution)/shard_map/ppermute | solution.py:99
  42.6 2.8 %collective-permute-start.10 = (f32[2,1,16,256]{3,2,0,1:T(8,128)S(1)}, f32[2,1,16,256]{3,2,0,1:T(8,128)S(1)}, u32[]{:S(2)}, u32[]{:S(2)}) collective-permute-start(f32[2,1,16,256]{3,2,0,1:T(8,128)S(1)} %get-tuple-element.65), channel_id=1, source_target_pairs={{0,11},{1,12},{2,13},{3,14},{4,15},{5,0},{6,1},{7,2},{8,3},{9,4},{... | collective-permute-start | bytes 98312 | tf_op jit(solution)/shard_map/ppermute | solution.py:99
  45.5 1.8 collective-permute-start.11
  48.1 4.6 %collective-permute-start.13 = (f32[2,1,16,256]{3,2,0,1:T(8,128)S(1)}, f32[2,1,16,256]{3,2,0,1:T(8,128)S(1)}, u32[]{:S(2)}, u32[]{:S(2)}) collective-permute-start(f32[2,1,16,256]{3,2,0,1:T(8,128)S(1)} %get-tuple-element.62), channel_id=1, source_target_pairs={{0,14},{1,15},{2,0},{3,1},{4,2},{5,3},{6,4},{7,5},{8,6},{9,7},{10,... | collective-permute-start | bytes 98312 | tf_op jit(solution)/shard_map/ppermute | solution.py:99
  52.7 4.1 %collective-permute-start.14 = (f32[2,1,16,256]{3,2,0,1:T(8,128)S(1)}, f32[2,1,16,256]{3,2,0,1:T(8,128)S(1)}, u32[]{:S(2)}, u32[]{:S(2)}) collective-permute-start(f32[2,1,16,256]{3,2,0,1:T(8,128)S(1)} %get-tuple-element.61), channel_id=1, source_target_pairs={{0,15},{1,0},{2,1},{3,2},{4,3},{5,4},{6,5},{7,6},{8,7},{9,8},{10,9... | collective-permute-start | bytes 98312 | tf_op jit(solution)/shard_map/ppermute | solution.py:99
  56.9 1.7 collective-permute-done.14
  64.0 2.5 %reshape.238 = f32[2,16,16,4,64]{4,3,2,1,0:T(4,128)} reshape(f32[2,16,16,256]{3,2,1,0:T(8,128)} %get-tuple-element.58) | data formatting | bytes 1048576 | tf_op jit(solution)/shard_map/reshape | solution.py:55
  69.3 3.1 %fusion.43 = (f32[2,16,4,16]{3,2,1,0:T(4,128)S(1)}, f32[2,16,4,16,16]{3,4,2,1,0:T(8,128)S(1)}) fusion(f32[2,16,16]{1,2,0:T(8,128)S(1)} %and_convert_fusion, f32[2,16,16,4,64]{4,3,2,1,0:T(4,128)S(1)} %get-tuple-element.84, f32[2,16,16,4,64]{4,3,2,1,0:T(4,128)S(1)} %get-tuple-element.85), kind=kOutput, calls=%fused_computation.114 | convolution fusion | flops 25262080 | bytes 1189888 | tf_op jit(solution)/shard_map/ctphd,csphd->cphts/dot_general | solution.py:56
  72.4 2.5 %fusion.18 = f32[2,16,16,4,64]{4,1,3,2,0:T(8,128)S(1)} fusion(f32[2,16,4,16,16]{3,4,2,1,0:T(8,128)S(1)} %get-tuple-element.77, f32[2,16,16,4,64]{4,3,2,1,0:T(4,128)S(1)} %copy-done.6, f32[2,16,16,4]{1,3,2,0:T(4,128)S(1)} %bitcast.215), kind=kOutput, calls=%fused_computation.30 | convolution fusion | flops 25296896 | bytes 1187840 | tf_op jit(solution)/shard_map/cphts,csphd->ctphd/dot_general | solution.py:67
  76.0 1.6 multiply_reduce_fusion.4
  77.9 9.9 %fusion.17 = (f32[512]{0:T(512)S(1)}, f32[512,4096]{1,0:T(8,128)S(1)}) fusion(f32[512,256]{1,0:T(8,128)S(1)} %bitcast_multiply_fusion.2, f32[4096,256]{1,0:T(8,128)} %all-gather.2.cloned.1.call-done), kind=kOutput, calls=%fused_computation.28 | convolution fusion | flops 6446644736 | bytes 13109248 | tf_op jit(solution)/shard_map/dot_general | solution.py:108
  87.8 3.2 %copy-done.1 = f32[512,4096]{1,0:T(8,128)} copy-done((f32[512,4096]{1,0:T(8,128)}, f32[512,4096]{1,0:T(8,128)S(1)}, u32[]{:S(2)}) %copy-start.1) | copy-done | bytes 8388632
  91.1 15.1 %fusion.31 = f32[4096,256]{1,0:T(8,128)} fusion(f32[512,256]{1,0:T(8,128)S(1)} %bitcast_multiply_fusion.2, f32[512,4096]{1,0:T(8,128)S(1)} %get-tuple-element.81, f32[512]{0:T(512)S(1)} %get-tuple-element.80), kind=kOutput, calls=%fused_computation.52 | convolution fusion | flops 6446645248 | bytes 13109248 | tf_op jit(solution)/shard_map/dot_general | solution.py:111
  107.4 4.3 %fusion.30 = f32[4096]{0:T(1024)S(1)} fusion(f32[512]{0:T(512)S(1)} %get-tuple-element.80, f32[512,4096]{1,0:T(8,128)} %copy-done.1), kind=kLoop, calls=%fused_computation.51 | loop fusion | flops 6287360 | bytes 8407040 | tf_op jit(solution)/shard_map/reduce_sum | solution.py:114
  111.7 63.3 %all-reduce = f32[4096]{0:T(1024)S(1)} all-reduce(f32[4096]{0:T(1024)S(1)} %fusion.30), channel_id=3, replica_groups=mesh['groups'=2,'frames'=16] {'frames'}, use_global_device_ids=true, to_apply=%region_15.16.clone | all-reduce | flops 4096 | bytes 32768
  175.1 6.4 %reduce-scatter.2.cloned.1.call-done = f32[256,256]{1,0:T(8,128)} async-done(((f32[4096,256]{1,0:T(8,128)}), f32[256,256]{1,0:T(8,128)}) %reduce-scatter.2.cloned.1.call-update) | async-done | bytes 262160 | tf_op jit(solution)/shard_map/reduce_scatter | solution.py:116
  181.5 1.8 broadcast_divide_fusion
  (121 shorter events, 28.2 us)
Async XLA Ops:
  7.2 52.2 %copy-start = (f32[256,768]{1,0:T(8,128)S(1)}, f32[256,768]{1,0:T(8,128)}, u32[]{:S(2)}) copy-start(f32[256,768]{1,0:T(8,128)} %param.18) | copy-start | bytes 2359300
  7.2 70.7 %all-gather.2.cloned.1.call-start = ((), (), s32[]{:S(2)}) async-start(), calls=%async_computation.1 | async-start | bytes 4456448 | tf_op jit(solution)/shard_map/all_gather | solution.py:106
  10.3 171.2 %reduce-scatter.2.cloned.1.call-start = ((), (), s32[]{:S(2)}) async-start(), calls=%async_computation.2 | async-start | bytes 4456448 | tf_op jit(solution)/shard_map/reduce_scatter | solution.py:116
  10.5 23.3 %copy-start.10 = (s32[2]{0:T(128)S(1)}, s32[2]{0:T(128)}, u32[]{:S(2)}) copy-start(s32[2]{0:T(128)} %param.13) | copy-start | bytes 28
  10.5 48.9 %copy-start.9 = (f32[256]{0:T(256)S(1)}, f32[256]{0:T(256)}, u32[]{:S(2)}) copy-start(f32[256]{0:T(256)} %param.17) | copy-start | bytes 3076
  25.7 8.3 %collective-permute-start = (f32[2,1,16,256]{3,2,0,1:T(8,128)S(1)}, f32[2,1,16,256]{3,2,0,1:T(8,128)S(1)}, u32[]{:S(2)}, u32[]{:S(2)}) collective-permute-start(f32[2,1,16,256]{3,2,0,1:T(8,128)S(1)} %get-tuple-element.75), channel_id=1, source_target_pairs={{0,1},{1,2},{2,3},{3,4},{4,5},{5,6},{6,7},{7,8},{8,9},{9,10},{10,1... | collective-permute-start | bytes 98312 | tf_op jit(solution)/shard_map/ppermute | solution.py:99
  26.2 9.0 %collective-permute-start.1 = (f32[2,1,16,256]{3,2,0,1:T(8,128)S(1)}, f32[2,1,16,256]{3,2,0,1:T(8,128)S(1)}, u32[]{:S(2)}, u32[]{:S(2)}) collective-permute-start(f32[2,1,16,256]{3,2,0,1:T(8,128)S(1)} %get-tuple-element.74), channel_id=1, source_target_pairs={{0,2},{1,3},{2,4},{3,5},{4,6},{5,7},{6,8},{7,9},{8,10},{9,11},{10,... | collective-permute-start | bytes 98312 | tf_op jit(solution)/shard_map/ppermute | solution.py:99
  28.8 10.7 %collective-permute-start.2 = (f32[2,1,16,256]{3,2,0,1:T(8,128)S(1)}, f32[2,1,16,256]{3,2,0,1:T(8,128)S(1)}, u32[]{:S(2)}, u32[]{:S(2)}) collective-permute-start(f32[2,1,16,256]{3,2,0,1:T(8,128)S(1)} %get-tuple-element.73), channel_id=1, source_target_pairs={{0,3},{1,4},{2,5},{3,6},{4,7},{5,8},{6,9},{7,10},{8,11},{9,12},{10... | collective-permute-start | bytes 98312 | tf_op jit(solution)/shard_map/ppermute | solution.py:99
  31.2 8.6 %collective-permute-start.3 = (f32[2,1,16,256]{3,2,0,1:T(8,128)S(1)}, f32[2,1,16,256]{3,2,0,1:T(8,128)S(1)}, u32[]{:S(2)}, u32[]{:S(2)}) collective-permute-start(f32[2,1,16,256]{3,2,0,1:T(8,128)S(1)} %get-tuple-element.72), channel_id=1, source_target_pairs={{0,4},{1,5},{2,6},{3,7},{4,8},{5,9},{6,10},{7,11},{8,12},{9,13},{1... | collective-permute-start | bytes 98312 | tf_op jit(solution)/shard_map/ppermute | solution.py:99
  32.8 7.4 %collective-permute-start.4 = (f32[2,1,16,256]{3,2,0,1:T(8,128)S(1)}, f32[2,1,16,256]{3,2,0,1:T(8,128)S(1)}, u32[]{:S(2)}, u32[]{:S(2)}) collective-permute-start(f32[2,1,16,256]{3,2,0,1:T(8,128)S(1)} %get-tuple-element.71), channel_id=1, source_target_pairs={{0,5},{1,6},{2,7},{3,8},{4,9},{5,10},{6,11},{7,12},{8,13},{9,14},{... | collective-permute-start | bytes 98312 | tf_op jit(solution)/shard_map/ppermute | solution.py:99
  34.0 8.7 %collective-permute-start.5 = (f32[2,1,16,256]{3,2,0,1:T(8,128)S(1)}, f32[2,1,16,256]{3,2,0,1:T(8,128)S(1)}, u32[]{:S(2)}, u32[]{:S(2)}) collective-permute-start(f32[2,1,16,256]{3,2,0,1:T(8,128)S(1)} %get-tuple-element.70), channel_id=1, source_target_pairs={{0,6},{1,7},{2,8},{3,9},{4,10},{5,11},{6,12},{7,13},{8,14},{9,15},... | collective-permute-start | bytes 98312 | tf_op jit(solution)/shard_map/ppermute | solution.py:99
  35.2 10.3 %collective-permute-start.6 = (f32[2,1,16,256]{3,2,0,1:T(8,128)S(1)}, f32[2,1,16,256]{3,2,0,1:T(8,128)S(1)}, u32[]{:S(2)}, u32[]{:S(2)}) collective-permute-start(f32[2,1,16,256]{3,2,0,1:T(8,128)S(1)} %get-tuple-element.69), channel_id=1, source_target_pairs={{0,7},{1,8},{2,9},{3,10},{4,11},{5,12},{6,13},{7,14},{8,15},{9,0},... | collective-permute-start | bytes 98312 | tf_op jit(solution)/shard_map/ppermute | solution.py:99
  39.5 8.6 %collective-permute-start.7 = (f32[2,1,16,256]{3,2,0,1:T(8,128)S(1)}, f32[2,1,16,256]{3,2,0,1:T(8,128)S(1)}, u32[]{:S(2)}, u32[]{:S(2)}) collective-permute-start(f32[2,1,16,256]{3,2,0,1:T(8,128)S(1)} %get-tuple-element.68), channel_id=1, source_target_pairs={{0,8},{1,9},{2,10},{3,11},{4,12},{5,13},{6,14},{7,15},{8,0},{9,1},... | collective-permute-start | bytes 98312 | tf_op jit(solution)/shard_map/ppermute | solution.py:99
  39.9 8.2 %collective-permute-start.8 = (f32[2,1,16,256]{3,2,0,1:T(8,128)S(1)}, f32[2,1,16,256]{3,2,0,1:T(8,128)S(1)}, u32[]{:S(2)}, u32[]{:S(2)}) collective-permute-start(f32[2,1,16,256]{3,2,0,1:T(8,128)S(1)} %get-tuple-element.67), channel_id=1, source_target_pairs={{0,9},{1,10},{2,11},{3,12},{4,13},{5,14},{6,15},{7,0},{8,1},{9,2},... | collective-permute-start | bytes 98312 | tf_op jit(solution)/shard_map/ppermute | solution.py:99
  40.2 12.6 %collective-permute-start.9 = (f32[2,1,16,256]{3,2,0,1:T(8,128)S(1)}, f32[2,1,16,256]{3,2,0,1:T(8,128)S(1)}, u32[]{:S(2)}, u32[]{:S(2)}) collective-permute-start(f32[2,1,16,256]{3,2,0,1:T(8,128)S(1)} %get-tuple-element.66), channel_id=1, source_target_pairs={{0,10},{1,11},{2,12},{3,13},{4,14},{5,15},{6,0},{7,1},{8,2},{9,3},... | collective-permute-start | bytes 98312 | tf_op jit(solution)/shard_map/ppermute | solution.py:99
  42.6 14.2 %collective-permute-start.10 = (f32[2,1,16,256]{3,2,0,1:T(8,128)S(1)}, f32[2,1,16,256]{3,2,0,1:T(8,128)S(1)}, u32[]{:S(2)}, u32[]{:S(2)}) collective-permute-start(f32[2,1,16,256]{3,2,0,1:T(8,128)S(1)} %get-tuple-element.65), channel_id=1, source_target_pairs={{0,11},{1,12},{2,13},{3,14},{4,15},{5,0},{6,1},{7,2},{8,3},{9,4},{... | collective-permute-start | bytes 98312 | tf_op jit(solution)/shard_map/ppermute | solution.py:99
  45.5 11.4 %collective-permute-start.11 = (f32[2,1,16,256]{3,2,0,1:T(8,128)S(1)}, f32[2,1,16,256]{3,2,0,1:T(8,128)S(1)}, u32[]{:S(2)}, u32[]{:S(2)}) collective-permute-start(f32[2,1,16,256]{3,2,0,1:T(8,128)S(1)} %get-tuple-element.64), channel_id=1, source_target_pairs={{0,12},{1,13},{2,14},{3,15},{4,0},{5,1},{6,2},{7,3},{8,4},{9,5},{1... | collective-permute-start | bytes 98312 | tf_op jit(solution)/shard_map/ppermute | solution.py:99
  48.1 8.8 %collective-permute-start.12 = (f32[2,1,16,256]{3,2,0,1:T(8,128)S(1)}, f32[2,1,16,256]{3,2,0,1:T(8,128)S(1)}, u32[]{:S(2)}, u32[]{:S(2)}) collective-permute-start(f32[2,1,16,256]{3,2,0,1:T(8,128)S(1)} %get-tuple-element.63), channel_id=1, source_target_pairs={{0,13},{1,14},{2,15},{3,0},{4,1},{5,2},{6,3},{7,4},{8,5},{9,6},{10... | collective-permute-start | bytes 98312 | tf_op jit(solution)/shard_map/ppermute | solution.py:99
  48.1 8.8 %collective-permute-start.13 = (f32[2,1,16,256]{3,2,0,1:T(8,128)S(1)}, f32[2,1,16,256]{3,2,0,1:T(8,128)S(1)}, u32[]{:S(2)}, u32[]{:S(2)}) collective-permute-start(f32[2,1,16,256]{3,2,0,1:T(8,128)S(1)} %get-tuple-element.62), channel_id=1, source_target_pairs={{0,14},{1,15},{2,0},{3,1},{4,2},{5,3},{6,4},{7,5},{8,6},{9,7},{10,... | collective-permute-start | bytes 98312 | tf_op jit(solution)/shard_map/ppermute | solution.py:99
  52.7 5.9 %collective-permute-start.14 = (f32[2,1,16,256]{3,2,0,1:T(8,128)S(1)}, f32[2,1,16,256]{3,2,0,1:T(8,128)S(1)}, u32[]{:S(2)}, u32[]{:S(2)}) collective-permute-start(f32[2,1,16,256]{3,2,0,1:T(8,128)S(1)} %get-tuple-element.61), channel_id=1, source_target_pairs={{0,15},{1,0},{2,1},{3,2},{4,3},{5,4},{6,5},{7,6},{8,7},{9,8},{10,9... | collective-permute-start | bytes 98312 | tf_op jit(solution)/shard_map/ppermute | solution.py:99
  77.6 28.5 %copy-start.5 = (f32[2,16,16,256]{3,2,1,0:T(8,128)}, f32[2,16,16,256]{3,2,1,0:T(8,128)S(1)}, u32[]{:S(2)}) copy-start(f32[2,16,16,256]{3,2,1,0:T(8,128)S(1)} %get-tuple-element.79) | copy-start | bytes 1572868
  91.1 15.1 %copy-start.11 = (u32[32]{0:T(128)S(1)}, u32[32]{0:T(128)}, u32[]{:S(2)}) copy-start(u32[32]{0:T(128)} %constant.157) | copy-start | bytes 388
  106.1 68.9 %copy-start.7 = (f32[256]{0:T(256)S(1)}, f32[256]{0:T(256)}, u32[]{:S(2)}) copy-start(f32[256]{0:T(256)} %param.21) | copy-start | bytes 3076
  106.1 75.4 %copy-start.4 = (f32[256,256]{1,0:T(8,128)S(1)}, f32[256,256]{1,0:T(8,128)}, u32[]{:S(2)}) copy-start(f32[256,256]{1,0:T(8,128)} %param.20) | copy-start | bytes 786436
  (7 other events, 40.3 us)
Sparse Core Ops, SparseCore 0:
  10.7 58.4 all-gather.1
  106.3 75.1 reduce-scatter.1
